TPU v7x, 128 devices: a whole 4x4x4 slice. The times are simulated.
128 devices in a mesh: corpus: 16 (over z, y), fsdp: 2 (over core), tensor: 4 (over x).
Axes of the slice: x: 4, y: 4, z: 4, core: 2. Of those that a mesh axis runs over, the one named last changes fastest.
Arguments:
- queries_in: bfloat16 [4096, 4096], P(('corpus', 'fsdp')), may hold values from -6 to 6
- head_weight: bfloat16 [4096, 4096], P('fsdp', 'tensor'), may hold values from -0.09375 to 0.09375
- passages: bfloat16 [16384, 4096], P('corpus', 'tensor'), may hold values from -0.15625 to 0.15625
- teacher: float32 [4096, 4, 32], P(('corpus', 'fsdp')), may hold values from -250 to 400
- cand_block: int32 [4096, 4], P(('corpus', 'fsdp')), may hold values from 0 to 127, all different within a row; in each aligned block of 128 rows (0 to 127, 128 to 255, ...) at most 6 rows name the same one
- cand_offset: int32 [4096, 4, 32], P(('corpus', 'fsdp')), may hold values from 0 to 127, as said below
- block_slot: int32 [128], replicated, may hold values from 0 to 127, each once
Outputs:
- kl_loss: float32 [4096], P(('corpus', 'fsdp'))
- head_grad: float32 [4096, 4096], P('fsdp', 'tensor')
Inputs may be any that keep to these rules, and one draw needn't show every extreme that they name: `cand_block`: in the rows of one device no block id appears more than 6 times, and some block id appears exactly 6 times there; the 4 ids of one query differ. `cand_offset`: the 32 offsets of one query in one block differ. `block_slot`: each storage position is taken by exactly one block.
All inputs are finite; a program needn't handle non-finite values.
Results may differ from a plain program's by a relative error of at most 0.012.
The roundings to bfloat16 on the way count: a program that leaves them out, or rounds other values in their place, can miss the bound.
Values may be sent and summed in bfloat16 or wider, within the bound.
A program may use at most 128 MiB of HBM per device.

v0:
```python
import jax
import jax.numpy as jnp
from jax import lax
from jax.sharding import PartitionSpec as P

ROWS = 128
MOSTB = 6


def on_device(queries_in, head_weight, passages, teacher, cand_block, cand_offset, block_slot):
    query_rows, model_width = queries_in.shape
    head_cols = head_weight.shape[1]
    per_query = cand_block.shape[1]
    offset_count = cand_offset.shape[2]
    total_blocks = block_slot.shape[0]
    n_corpus = lax.axis_size("corpus")
    blocks_here = passages.shape[0] // ROWS
    capacity = MOSTB
    slot_total = total_blocks * capacity
    columns = queries_in
    query = jnp.dot(
        columns,
        lax.all_gather(head_weight, "fsdp", axis=0, tiled=True),
        preferred_element_type=jnp.float32,
    ).astype(jnp.bfloat16)
    block_ids = lax.broadcasted_iota(jnp.int32, (1, total_blocks), 1)
    named = (cand_block.reshape(-1, 1) == block_ids).astype(jnp.int32)
    slot_of = jnp.sum(named * block_slot.reshape(1, -1), axis=1)
    slot_hits = (slot_of[:, None] == block_ids).astype(jnp.int32)
    slot_rank = jnp.sum((jnp.cumsum(slot_hits, axis=0) - slot_hits) * slot_hits, axis=1)
    position = slot_of * capacity + slot_rank
    query_copies = jnp.repeat(query, per_query, axis=0)
    send_queries = jnp.zeros((slot_total, head_cols), jnp.bfloat16).at[position].set(query_copies)
    send_queries = send_queries.reshape(n_corpus, blocks_here, capacity, head_cols)
    offset_rows = cand_offset.reshape(-1, offset_count)
    send_offsets = jnp.zeros((slot_total, offset_count), jnp.int32).at[position].set(offset_rows)
    send_offsets = send_offsets.reshape(n_corpus, blocks_here, capacity, offset_count)
    embedded = passages.reshape(blocks_here, ROWS, head_cols)
    scores = jnp.einsum(
        "sjmd,jrd->sjmr",
        lax.all_to_all(send_queries, "corpus", split_axis=0, concat_axis=0, tiled=True),
        embedded,
        preferred_element_type=jnp.float32,
    )
    returned_scores = lax.all_to_all(scores, "corpus", split_axis=0, concat_axis=0, tiled=True)
    picked = returned_scores.reshape(slot_total, ROWS)[position].reshape(
        query_rows, per_query, ROWS
    )
    partial_scores = jnp.take_along_axis(picked, cand_offset, axis=2)
    student = 50.0 * lax.psum(partial_scores, "tensor")
    log_student = student - jax.nn.logsumexp(student, axis=(1, 2), keepdims=True)
    log_teacher = teacher - jax.nn.logsumexp(teacher, axis=(1, 2), keepdims=True)
    prob_teacher = jnp.exp(log_teacher)
    kl_loss = jnp.sum(prob_teacher * (log_teacher - log_student), axis=(1, 2))
    dscore = (50.0 * (jnp.exp(log_student) - prob_teacher)).astype(jnp.bfloat16)
    flat_index = (position[:, None] * ROWS + offset_rows).reshape(-1)
    dense_grad = (
        jnp.zeros((slot_total * ROWS,), jnp.bfloat16).at[flat_index].set(dscore.reshape(-1))
    )
    dense_grad = dense_grad.reshape(n_corpus, blocks_here, capacity, ROWS)
    block_part = jnp.einsum(
        "sjmr,jrd->sjmd",
        lax.all_to_all(dense_grad, "corpus", split_axis=0, concat_axis=0, tiled=True),
        embedded,
        preferred_element_type=jnp.float32,
    ).astype(jnp.bfloat16)
    arrived_parts = lax.all_to_all(block_part, "corpus", split_axis=0, concat_axis=0, tiled=True)
    parts = arrived_parts.reshape(slot_total, head_cols)[position].reshape(
        query_rows, per_query, head_cols
    )
    query_grad = jnp.sum(parts.astype(jnp.float32), axis=1).astype(jnp.bfloat16)
    columns = queries_in
    grad_share = lax.psum_scatter(
        lax.dot_general(
            columns, query_grad, (((0,), (0,)), ((), ())), preferred_element_type=jnp.float32
        ),
        "fsdp",
        scatter_dimension=0,
        tiled=True,
    )
    head_grad = lax.psum(grad_share, "corpus")
    return (kl_loss, head_grad)


def solution(mesh):
    placed = (
        P(("corpus", "fsdp"), None),
        P("fsdp", "tensor"),
        P("corpus", "tensor"),
        P(("corpus", "fsdp"), None, None),
        P(("corpus", "fsdp"), None),
        P(("corpus", "fsdp"), None, None),
        P(),
    )
    return jax.shard_map(
        on_device,
        mesh=mesh,
        in_specs=placed,
        out_specs=(P(("corpus", "fsdp")), P("fsdp", "tensor")),
        check_vma=False,
    )
```

profile of v0, /device:TPU:0, one launch (start us, length us, event | category | flops | bytes accessed | tf_op | source)
XLA Modules:
  0.0 656.1 jit_solution(10483691207682673269)
XLA Ops:
  7.2 0.0 copy-start
  7.2 0.0 copy-start.1
  7.2 0.0 all-gather.2.cloned.1.call-start
  7.3 0.7 all-gather.2.cloned.1.call-update
  8.0 0.1 copy-done.6
  8.0 0.1 copy.59
  8.1 0.1 eq.38
  8.2 0.2 select_reduce_fusion
  8.5 0.1 copy.60
  8.6 0.2 fusion.10
  8.9 0.2 fusion.9
  9.2 0.1 add.96
  9.3 0.2 add.97
  9.5 0.1 copy.68
  9.6 0.8 reshape.163
  10.5 24.3 %all-gather.2.cloned.1.call-done = bf16[4096,1024]{1,0:T(8,128)(2,1)} async-done(((bf16[2048,1024]{1,0:T(8,128)(2,1)}), bf16[4096,1024]{1,0:T(8,128)(2,1)}) %all-gather.2.cloned.1.call-update) | async-done | bytes 8388624 | tf_op jit(solution)/shard_map/all_gather | solution.py:23
  34.7 4.6 convolution_convert_fusion.1
  39.4 0.3 broadcast_in_dim.11
  39.7 1.1 reshape.194
  40.8 4.5 scatter_custom_fusion
  45.3 3.7 reshape.158
  49.0 3.8 copy.62
  52.8 7.1 %all-to-all-start = ((bf16[16,8,6,1024]{3,1,2,0:T(8,128)(2,1)}), bf16[16,8,6,1024]{3,1,2,0:T(8,128)(2,1)}, u32[]{:S(2)}, u32[]{:S(2)}) async-start(bf16[16,8,6,1024]{3,1,2,0:T(8,128)(2,1)} %copy.62), calls=%async_computation | async-start | bytes 3145728 | tf_op jit(solution)/shard_map/all_to_all | solution.py:41
  59.9 0.7 compare_select_fusion
  60.6 24.8 %all-to-all-done = bf16[16,8,6,1024]{3,1,2,0:T(8,128)(2,1)} async-done(((bf16[16,8,6,1024]{3,1,2,0:T(8,128)(2,1)}), bf16[16,8,6,1024]{3,1,2,0:T(8,128)(2,1)}, u32[]{:S(2)}, u32[]{:S(2)}) %all-to-all-start) | async-done | bytes 1572896 | tf_op jit(solution)/shard_map/all_to_all | solution.py:41
  85.4 2.6 fusion.3
  88.1 1.0 copy.64
  89.0 3.6 all-to-all-start.1
  92.6 0.0 all-reduce.3.cloned.1.call-start
  92.7 0.1 copy.66
  92.8 0.2 reshape.184
  93.1 9.3 %all-to-all-done.1 = f32[16,8,6,128]{3,1,2,0:T(8,128)S(1)} async-done(((f32[16,8,6,128]{3,1,2,0:T(8,128)}), f32[16,8,6,128]{3,1,2,0:T(8,128)S(1)}, u32[]{:S(2)}, u32[]{:S(2)}) %all-to-all-start.1) | async-done | bytes 393248 | tf_op jit(solution)/shard_map/all_to_all | solution.py:45
  102.4 0.1 copy.65
  102.6 1.0 gather_fusion
  103.6 145.8 %gather_fusion.2 = f32[16384]{0:T(1024)S(1)} fusion(f32[128,4,128]{2,1,0:T(4,128)S(1)} %bitcast.43, s32[16384]{0:T(1024)S(1)} %reshape.184), kind=kCustom, calls=%fused_computation.2 | custom fusion | bytes 327680 | tf_op jit(solution)/shard_map/jit(take_along_axis)/gather | solution.py:49
  249.5 0.2 reshape.187
  249.6 0.1 copy.67
  249.8 0.6 and_select_fusion
  250.4 0.0 all-reduce.3.cloned.1.call-update
  250.4 0.2 reduce-scatter.2.cloned.1.call-start
  250.7 38.4 %all-reduce.3.cloned.1.call-done = f32[128,4,32]{0,2,1:T(8,128)} async-done(((f32[128,4,32]{0,2,1:T(8,128)}), f32[128,4,32]{0,2,1:T(8,128)}) %all-reduce.3.cloned.1.call-update) | async-done | bytes 65552 | tf_op jit(solution)/shard_map/psum | solution.py:50
  289.1 0.9 multiply_reduce_fusion.1
  289.9 0.9 exponential_reduce_fusion
  290.8 1.4 multiply_convert_fusion
  292.2 0.1 copy.69
  292.4 0.1 reshape.202
  292.5 112.7 %scatter_custom_fusion.1 = bf16[98304]{0:T(1024)(128)(2,1)S(1)} fusion(s32[16384]{0:T(1024)} %bitcast.46, bf16[16384]{0:T(1024)(128)(2,1)S(1)} %reshape.202, bf16[]{:T(256)} %constant.17.clone.1), kind=kCustom, calls=%fused_computation.28 | custom fusion | bytes 197120 | tf_op jit(solution)/shard_map/scatter | solution.py:58
  405.2 0.1 reshape.165
  405.4 15.1 %all_to_all.20 = bf16[16,8,6,128]{3,1,2,0:T(8,128)(2,1)S(1)} all-to-all(bf16[16,8,6,128]{3,1,2,0:T(8,128)(2,1)S(1)} %copy.70), channel_id=1, replica_groups=mesh['corpus'=16,'fsdp'=2,'tensor'=4] {'corpus'}, dimensions={0} | all-to-all | bytes 393216 | tf_op jit(solution)/shard_map/all_to_all | solution.py:63
  420.5 0.6 fusion.2
  421.0 0.9 copy.72
  421.9 22.4 %all_to_all.21 = bf16[16,8,6,1024]{3,1,2,0:T(8,128)(2,1)S(1)} all-to-all(bf16[16,8,6,1024]{3,1,2,0:T(8,128)(2,1)S(1)} %copy.72), channel_id=1, replica_groups=mesh['corpus'=16,'fsdp'=2,'tensor'=4] {'corpus'}, dimensions={0} | all-to-all | bytes 3145728 | tf_op jit(solution)/shard_map/all_to_all | solution.py:67
  444.3 2.4 copy.73
  446.7 3.7 reshape.166
  450.5 5.1 gather_fusion.1
  455.6 2.3 reshape.167
  457.9 2.5 reduce_sum.62
  460.4 8.1 %convolution_bitcast_fusion = f32[4096,1024]{0,1:T(8,128)} fusion(bf16[128,1024]{1,0:T(8,128)(2,1)S(1)} %reduce_sum.62, bf16[128,4096]{1,0:T(8,128)(2,1)S(1)} %copy-done.2), kind=kOutput, calls=%fused_computation.5 | convolution fusion | flops 1073741824 | bytes 18087936 | tf_op jit(solution)/shard_map/dot_general | solution.py:74
  468.5 0.0 reduce-scatter.2.cloned.1.call-update
  468.5 0.0 all-reduce.5.cloned.1.call-start
  468.6 24.9 %reduce-scatter.2.cloned.1.call-done = f32[2048,1024]{0,1:T(8,128)} async-done(((f32[4096,1024]{0,1:T(8,128)}), f32[2048,1024]{0,1:T(8,128)}) %reduce-scatter.2.cloned.1.call-update) | async-done | bytes 8388624 | tf_op jit(solution)/shard_map/reduce_scatter | solution.py:73
  493.5 0.0 all-reduce.5.cloned.1.call-update
  493.5 146.8 %all-reduce.5.cloned.1.call-done = f32[2048,1024]{0,1:T(8,128)} async-done(((f32[2048,1024]{0,1:T(8,128)}), f32[2048,1024]{0,1:T(8,128)}) %all-reduce.5.cloned.1.call-update) | async-done | bytes 8388624 | tf_op jit(solution)/shard_map/psum | solution.py:81
  640.4 9.2 %copy.74 = f32[2048,1024]{1,0:T(8,128)} copy(f32[2048,1024]{0,1:T(8,128)} %all-reduce.5.cloned.1.call-done) | data formatting | bytes 16777216
  (31 shorter events, 0.3 us)
Async XLA Ops:
  7.2 78.2 %copy-start = (bf16[1024,1024]{1,0:T(8,128)(2,1)S(1)}, bf16[1024,1024]{1,0:T(8,128)(2,1)}, u32[]{:S(2)}) copy-start(bf16[1024,1024]{1,0:T(8,128)(2,1)} %param.9) | copy-start | bytes 6291460
  7.2 0.8 copy-start.6
  7.2 1.0 copy-start.7
  7.2 2.3 copy-start.3
  7.2 27.5 %copy-start.1 = (bf16[128,4096]{1,0:T(8,128)(2,1)S(1)}, bf16[128,4096]{1,0:T(8,128)(2,1)}, u32[]{:S(2)}) copy-start(bf16[128,4096]{1,0:T(8,128)(2,1)} %param.7) | copy-start | bytes 3145732
  7.2 27.5 %all-gather.2.cloned.1.call-start = ((), (), s32[]{:S(2)}) async-start(), calls=%async_computation.5 | async-start | bytes 12582912 | tf_op jit(solution)/shard_map/all_gather | solution.py:23
  49.0 10.9 %copy-start.5 = (s32[16384,1]{0,1:T(1,128)S(1)}, s32[16384,1]{0,1:T(1,128)}, u32[]{:S(2)}) copy-start(s32[16384,1]{0,1:T(1,128)} %reshape.163) | copy-start | bytes 196612
  52.8 32.6 %all-to-all-start = ((bf16[16,8,6,1024]{3,1,2,0:T(8,128)(2,1)}), bf16[16,8,6,1024]{3,1,2,0:T(8,128)(2,1)}, u32[]{:S(2)}, u32[]{:S(2)}) async-start(bf16[16,8,6,1024]{3,1,2,0:T(8,128)(2,1)} %copy.62), calls=%async_computation | async-start | bytes 3145728 | tf_op jit(solution)/shard_map/all_to_all | solution.py:41
  85.4 7.6 %copy-start.4 = (f32[128,4,32]{0,2,1:T(8,128)S(1)}, f32[128,4,32]{0,2,1:T(8,128)}, u32[]{:S(2)}) copy-start(f32[128,4,32]{0,2,1:T(8,128)} %param.10) | copy-start | bytes 196612
  89.0 13.4 %all-to-all-start.1 = ((f32[16,8,6,128]{3,1,2,0:T(8,128)}), f32[16,8,6,128]{3,1,2,0:T(8,128)S(1)}, u32[]{:S(2)}, u32[]{:S(2)}) async-start(f32[16,8,6,128]{3,1,2,0:T(8,128)} %copy.64), calls=%async_computation.1 | async-start | bytes 786432 | tf_op jit(solution)/shard_map/all_to_all | solution.py:45
  92.6 196.5 %all-reduce.3.cloned.1.call-start = ((), (), s32[]{:S(2)}) async-start(), calls=%async_computation.6 | async-start | bytes 131072 | tf_op jit(solution)/shard_map/psum | solution.py:50
  250.4 243.1 %reduce-scatter.2.cloned.1.call-start = ((), (), s32[]{:S(2)}) async-start(), calls=%async_computation.7 | async-start | bytes 25165824 | tf_op jit(solution)/shard_map/reduce_scatter | solution.py:73
  455.6 4.9 copy-start.2
  468.5 171.8 %all-reduce.5.cloned.1.call-start = ((), (), s32[]{:S(2)}) async-start(), calls=%async_computation.8 | async-start | bytes 16777216 | tf_op jit(solution)/shard_map/psum | solution.py:81
Sparse Core Ops, SparseCore 0:
  9.7 25.0 all-gather.1
  250.6 38.4 all-reduce.2
  468.6 24.7 reduce-scatter.1
  497.0 143.3 all-reduce.4
where the time goes:
time: 657 us; the launch traced here: 656 us
  local copies, waits for them, and re-layouts  300 us (46%)
  waiting for transfers between devices  269 us (41%)
  blocking collectives  37.5 us (6%)
  matrix products  15.9 us (2%)
  between operations  14.1 us (2%)
  starting transfers between devices  11 us (2%)
  other arithmetic  7.89 us (1%)
    psum x1, waiting for transfers between devices, on_device(): head_grad = lax.psum(grad_share, 'corpus')  147 us
    gather x5, local copies, waits for them, and re-layouts, on_device(): partial_scores = jnp.take_along_axis(picked, cand_offset, axis=2)  146 us
    scatter x1, local copies, waits for them, and re-layouts, on_device(): jnp.zeros((slot_total * ROWS,), jnp.bfloat16).at[flat_index]  113 us
    psum x1, waiting for transfers between devices, on_device(): student = 50.0 * lax.psum(partial_scores, 'tensor')  38.4 us
    reduce_scatter x1, waiting for transfers between devices, on_device(): lax.psum_scatter(lax.dot_general(columns, query_grad, (((0,), (0,)), ((),...  24.9 us
    all_to_all x1, waiting for transfers between devices, on_device(): lax.all_to_all(send_queries, 'corpus', split_axis=0, concat_axis=0, tiled...  24.8 us
    all_gather x1, waiting for transfers between devices, on_device(): lax.all_gather(head_weight, 'fsdp', axis=0, tiled=True)  24.3 us
    all_to_all x1, blocking collectives, on_device(): lax.all_to_all(block_part, 'corpus', split_axis=0, concat_axis=0, tiled=T...  22.4 us
  transfers between devices with their start and end apart: 6, of which 6 were waited for; matrix products, arithmetic and copies ran while one was open for 1% of the time, Pallas kernels for 0%

commit v1 on v0

--- a/solution.py
+++ b/solution.py
@@ -47,7 +47,7 @@
         query_rows, per_query, ROWS
     )
     partial_scores = jnp.take_along_axis(picked, cand_offset, axis=2)
-    student = 50.0 * lax.psum(partial_scores, "tensor")
+    student = 50.0 * jnp.sum(lax.all_gather(partial_scores, "tensor"), axis=0)
     log_student = student - jax.nn.logsumexp(student, axis=(1, 2), keepdims=True)
     log_teacher = teacher - jax.nn.logsumexp(teacher, axis=(1, 2), keepdims=True)
     prob_teacher = jnp.exp(log_teacher)

time: 657 us -> 623 us (0.948)
  waiting for transfers between devices: 269 us -> 231 us
  blocking collectives: 37.5 us -> 44.5 us
    psum x1 -> x0, waiting for transfers between devices: 38.4 us -> none  [on_device(): student = 50.0 * lax.psum(partial_scores, 'tensor')]
    all_gather x0 -> x1, blocking collectives: none -> 12.9 us  [on_device(): student = 50.0 * jnp.sum(lax.all_gather(partial_scores, 'tensor'), axis=0)]
  transfers between devices with their start and end apart: 6 -> 5, of which waited for: 6 -> 5; matrix products, arithmetic and copies ran while one was open for 1% -> 1% of each run, Pallas kernels for 0% -> 0%
where the time goes in v1:
time: 623 us
  local copies, waits for them, and re-layouts  301 us (48%)
  waiting for transfers between devices  231 us (37%)
  blocking collectives  44.5 us (7%)
  matrix products  15.9 us (3%)
  between operations  14.1 us (2%)
  starting transfers between devices  10.8 us (2%)
    psum x1, waiting for transfers between devices, on_device(): head_grad = lax.psum(grad_share, 'corpus')  147 us
    gather x5, local copies, waits for them, and re-layouts, on_device(): partial_scores = jnp.take_along_axis(picked, cand_offset, axis=2)  146 us
    scatter x1, local copies, waits for them, and re-layouts, on_device(): jnp.zeros((slot_total * ROWS,), jnp.bfloat16).at[flat_index]  113 us
    reduce_scatter x1, waiting for transfers between devices, on_device(): lax.psum_scatter(lax.dot_general(columns, query_grad, (((0,), (0,)), ((),...  25.1 us
    all_to_all x1, waiting for transfers between devices, on_device(): lax.all_to_all(send_queries, 'corpus', split_axis=0, concat_axis=0, tiled...  24.8 us
    all_gather x1, waiting for transfers between devices, on_device(): lax.all_gather(head_weight, 'fsdp', axis=0, tiled=True)  24.3 us
    all_to_all x1, blocking collectives, on_device(): lax.all_to_all(block_part, 'corpus', split_axis=0, concat_axis=0, tiled=T...  20.2 us
    all_gather x1, blocking collectives, on_device(): student = 50.0 * jnp.sum(lax.all_gather(partial_scores, 'tensor'), axis=0)  12.9 us
  transfers between devices with their start and end apart: 5, of which 5 were waited for; matrix products, arithmetic and copies ran while one was open for 1% of the time, Pallas kernels for 0%

profile of v1, /device:TPU:0, one launch (start us, length us, event | category | flops | bytes accessed | tf_op | source)
XLA Modules:
  0.0 622.5 jit_solution(5066638519514712175)
XLA Ops:
  7.2 0.0 copy-start
  7.2 0.0 copy-start.6
  7.2 0.0 copy-start.1
  7.2 0.0 all-gather.3.cloned.1.call-start
  7.3 0.7 all-gather.3.cloned.1.call-update
  8.0 0.1 copy-done.6
  8.0 0.1 copy.63
  8.1 0.1 eq.38
  8.2 0.2 select_reduce_fusion
  8.5 0.1 copy.64
  8.6 0.2 fusion.10
  8.9 0.2 fusion.9
  9.2 0.1 add.94
  9.3 0.2 add.95
  9.5 0.0 copy-done.3
  9.5 0.1 copy.74
  9.6 0.8 reshape.166
  10.5 24.3 %all-gather.3.cloned.1.call-done = bf16[4096,1024]{1,0:T(8,128)(2,1)} async-done(((bf16[2048,1024]{1,0:T(8,128)(2,1)}), bf16[4096,1024]{1,0:T(8,128)(2,1)}) %all-gather.3.cloned.1.call-update) | async-done | bytes 8388624 | tf_op jit(solution)/shard_map/all_gather | solution.py:23
  34.7 4.6 convolution_convert_fusion.1
  39.4 0.3 broadcast_in_dim.11
  39.7 1.1 reshape.197
  40.8 4.5 scatter_custom_fusion
  45.3 3.7 reshape.161
  49.0 3.8 copy.66
  52.8 7.1 %all-to-all-start = ((bf16[16,8,6,1024]{3,1,2,0:T(8,128)(2,1)}), bf16[16,8,6,1024]{3,1,2,0:T(8,128)(2,1)}, u32[]{:S(2)}, u32[]{:S(2)}) async-start(bf16[16,8,6,1024]{3,1,2,0:T(8,128)(2,1)} %copy.66), calls=%async_computation | async-start | bytes 3145728 | tf_op jit(solution)/shard_map/all_to_all | solution.py:41
  59.9 0.7 compare_select_fusion
  60.6 24.8 %all-to-all-done = bf16[16,8,6,1024]{3,1,2,0:T(8,128)(2,1)} async-done(((bf16[16,8,6,1024]{3,1,2,0:T(8,128)(2,1)}), bf16[16,8,6,1024]{3,1,2,0:T(8,128)(2,1)}, u32[]{:S(2)}, u32[]{:S(2)}) %all-to-all-start) | async-done | bytes 1572896 | tf_op jit(solution)/shard_map/all_to_all | solution.py:41
  85.4 2.6 fusion.3
  88.1 1.0 copy.68
  89.0 3.6 all-to-all-start.1
  92.6 0.0 reduce-scatter.2.cloned.1.call-start
  92.7 0.1 copy.70
  92.8 0.2 reshape.187
  93.1 9.3 %all-to-all-done.1 = f32[16,8,6,128]{3,1,2,0:T(8,128)S(1)} async-done(((f32[16,8,6,128]{3,1,2,0:T(8,128)}), f32[16,8,6,128]{3,1,2,0:T(8,128)S(1)}, u32[]{:S(2)}, u32[]{:S(2)}) %all-to-all-start.1) | async-done | bytes 393248 | tf_op jit(solution)/shard_map/all_to_all | solution.py:45
  102.4 0.1 copy.69
  102.6 1.0 gather_fusion
  103.6 145.8 %gather_fusion.2 = f32[16384]{0:T(1024)S(1)} fusion(f32[128,4,128]{2,1,0:T(4,128)S(1)} %bitcast.44, s32[16384]{0:T(1024)S(1)} %reshape.187), kind=kCustom, calls=%fused_computation.2 | custom fusion | bytes 327680 | tf_op jit(solution)/shard_map/jit(take_along_axis)/gather | solution.py:49
  249.5 0.2 reshape.190
  249.6 0.1 copy.71
  249.8 12.9 %all-gather = f32[512,4,32]{0,2,1:T(8,128)S(1)} all-gather(f32[128,4,32]{0,2,1:T(8,128)S(1)} %and_select_fusion), channel_id=2, replica_groups=mesh['corpus'=16,'fsdp'=2,'tensor'=4] {'tensor'}, dimensions={0}, use_global_device_ids=true | all-gather | bytes 327680 | tf_op jit(solution)/shard_map/all_gather | solution.py:50
  262.6 0.4 copy.82
  263.0 0.3 reduce_sum.69
  263.4 0.1 copy.73
  263.6 0.6 multiply_convert_fusion
  264.2 0.1 copy.75
  264.3 0.1 reshape.205
  264.4 112.7 %scatter_custom_fusion.1 = bf16[98304]{0:T(1024)(128)(2,1)S(1)} fusion(s32[16384]{0:T(1024)} %bitcast.48, bf16[16384]{0:T(1024)(128)(2,1)S(1)} %reshape.205, bf16[]{:T(256)} %constant.17.clone.1), kind=kCustom, calls=%fused_computation.28 | custom fusion | bytes 197120 | tf_op jit(solution)/shard_map/scatter | solution.py:58
  377.2 0.1 reshape.168
  377.3 11.5 %all_to_all.20 = bf16[16,8,6,128]{3,1,2,0:T(8,128)(2,1)S(1)} all-to-all(bf16[16,8,6,128]{3,1,2,0:T(8,128)(2,1)S(1)} %copy.76), channel_id=1, replica_groups=mesh['corpus'=16,'fsdp'=2,'tensor'=4] {'corpus'}, dimensions={0} | all-to-all | bytes 393216 | tf_op jit(solution)/shard_map/all_to_all | solution.py:63
  388.7 0.6 fusion.2
  389.3 0.9 copy.78
  390.2 20.2 %all_to_all.21 = bf16[16,8,6,1024]{3,1,2,0:T(8,128)(2,1)S(1)} all-to-all(bf16[16,8,6,1024]{3,1,2,0:T(8,128)(2,1)S(1)} %copy.78), channel_id=1, replica_groups=mesh['corpus'=16,'fsdp'=2,'tensor'=4] {'corpus'}, dimensions={0} | all-to-all | bytes 3145728 | tf_op jit(solution)/shard_map/all_to_all | solution.py:67
  410.4 2.4 copy.79
  412.8 3.7 reshape.169
  416.5 5.1 gather_fusion.1
  421.6 2.3 reshape.170
  423.9 2.5 reduce_sum.72
  426.4 8.1 %convolution_bitcast_fusion = f32[4096,1024]{0,1:T(8,128)} fusion(bf16[128,1024]{1,0:T(8,128)(2,1)S(1)} %reduce_sum.72, bf16[128,4096]{1,0:T(8,128)(2,1)S(1)} %copy-done.2), kind=kOutput, calls=%fused_computation.5 | convolution fusion | flops 1073741824 | bytes 18087936 | tf_op jit(solution)/shard_map/dot_general | solution.py:74
  434.5 0.0 reduce-scatter.2.cloned.1.call-update
  434.6 0.0 all-reduce.2.cloned.1.call-start
  434.6 25.1 %reduce-scatter.2.cloned.1.call-done = f32[2048,1024]{0,1:T(8,128)} async-done(((f32[4096,1024]{0,1:T(8,128)}), f32[2048,1024]{0,1:T(8,128)}) %reduce-scatter.2.cloned.1.call-update) | async-done | bytes 8388624 | tf_op jit(solution)/shard_map/reduce_scatter | solution.py:73
  459.7 0.0 all-reduce.2.cloned.1.call-update
  459.7 147.0 %all-reduce.2.cloned.1.call-done = f32[2048,1024]{0,1:T(8,128)} async-done(((f32[2048,1024]{0,1:T(8,128)}), f32[2048,1024]{0,1:T(8,128)}) %all-reduce.2.cloned.1.call-update) | async-done | bytes 8388624 | tf_op jit(solution)/shard_map/psum | solution.py:81
  606.8 9.2 %copy.80 = f32[2048,1024]{1,0:T(8,128)} copy(f32[2048,1024]{0,1:T(8,128)} %all-reduce.2.cloned.1.call-done) | data formatting | bytes 16777216
  (31 shorter events, 0.5 us)
Async XLA Ops:
  7.2 78.2 %copy-start = (bf16[1024,1024]{1,0:T(8,128)(2,1)S(1)}, bf16[1024,1024]{1,0:T(8,128)(2,1)}, u32[]{:S(2)}) copy-start(bf16[1024,1024]{1,0:T(8,128)(2,1)} %param.9) | copy-start | bytes 6291460
  7.2 0.8 copy-start.6
  7.2 1.0 copy-start.7
  7.2 2.3 copy-start.3
  7.2 27.5 %copy-start.1 = (bf16[128,4096]{1,0:T(8,128)(2,1)S(1)}, bf16[128,4096]{1,0:T(8,128)(2,1)}, u32[]{:S(2)}) copy-start(bf16[128,4096]{1,0:T(8,128)(2,1)} %param.7) | copy-start | bytes 3145732
  7.2 27.5 %all-gather.3.cloned.1.call-start = ((), (), s32[]{:S(2)}) async-start(), calls=%async_computation.5 | async-start | bytes 12582912 | tf_op jit(solution)/shard_map/all_gather | solution.py:23
  49.0 10.9 %copy-start.5 = (s32[16384,1]{0,1:T(1,128)S(1)}, s32[16384,1]{0,1:T(1,128)}, u32[]{:S(2)}) copy-start(s32[16384,1]{0,1:T(1,128)} %reshape.166) | copy-start | bytes 196612
  52.8 32.6 %all-to-all-start = ((bf16[16,8,6,1024]{3,1,2,0:T(8,128)(2,1)}), bf16[16,8,6,1024]{3,1,2,0:T(8,128)(2,1)}, u32[]{:S(2)}, u32[]{:S(2)}) async-start(bf16[16,8,6,1024]{3,1,2,0:T(8,128)(2,1)} %copy.66), calls=%async_computation | async-start | bytes 3145728 | tf_op jit(solution)/shard_map/all_to_all | solution.py:41
  85.4 7.6 %copy-start.4 = (f32[128,4,32]{0,2,1:T(8,128)S(1)}, f32[128,4,32]{0,2,1:T(8,128)}, u32[]{:S(2)}) copy-start(f32[128,4,32]{0,2,1:T(8,128)} %param.10) | copy-start | bytes 196612
  89.0 13.4 %all-to-all-start.1 = ((f32[16,8,6,128]{3,1,2,0:T(8,128)}), f32[16,8,6,128]{3,1,2,0:T(8,128)S(1)}, u32[]{:S(2)}, u32[]{:S(2)}) async-start(f32[16,8,6,128]{3,1,2,0:T(8,128)} %copy.68), calls=%async_computation.1 | async-start | bytes 786432 | tf_op jit(solution)/shard_map/all_to_all | solution.py:45
  92.6 367.1 %reduce-scatter.2.cloned.1.call-start = ((), (), s32[]{:S(2)}) async-start(), calls=%async_computation.6 | async-start | bytes 25165824 | tf_op jit(solution)/shard_map/reduce_scatter | solution.py:73
  421.6 4.9 copy-start.2
  434.6 172.2 %all-reduce.2.cloned.1.call-start = ((), (), s32[]{:S(2)}) async-start(), calls=%async_computation.7 | async-start | bytes 16777216 | tf_op jit(solution)/shard_map/psum | solution.py:81
Sparse Core Ops, SparseCore 0:
  9.7 25.0 all-gather.2
  434.7 24.9 reduce-scatter.1
  463.3 143.3 all-reduce.1
